TPU v7x, 32 devices: a whole 2x2x4 slice. The times are simulated.
32 devices in a mesh: row: 4 (over x, core), col: 4 (over z), vir: 2 (over y).
Axes of the slice: x: 2, y: 2, z: 4, core: 2. Of those that a mesh axis runs over, the one named last changes fastest.
Arguments:
- amplitudes: float32 [80, 4, 4, 3, 128, 128], P('vir', 'row', 'col'), may hold values from -6 to 6
- integrals: float32 [80, 4, 4, 3, 128, 128], P('vir', 'row', 'col'), may hold values from -6 to 6
- cycle_terms: float32 [80, 4, 4, 3, 128, 128], P('vir', 'row', 'col'), may hold values from -0.15625 to 0.15625
- ladder_factors: float32 [80, 8, 128, 128], P('vir'), may hold values from -0.375 to 0.375
- live: int32 [80, 4, 4, 3], P('vir', 'row', 'col'), may hold values 0 or 1
Outputs:
- residual: float32 [80, 4, 4, 3, 128, 128], P('vir', 'row', 'col')
All inputs are finite; a program needn't handle non-finite values. No bound on the sum of `live` on one device may be relied on, other than what follows from the above.
Results may differ from a plain program's by a relative error of at most 0.0001.
Values sent between devices are 32-bit elements; how exact they have to be, the bound alone decides.
No kernel may reach another device: no remote copies, remote signals or barrier semaphores. Data moves between devices by JAX's collectives and lax.ppermute only.
A program may use at most 448 MiB of HBM per device.

v0:
```python
import jax
import jax.numpy as jnp
from jax import lax
from jax.sharding import PartitionSpec as P

NT = 80


def extended(block, sides, width):
    for axis, dim in sides:
        count = lax.axis_size(axis)
        forward = [(i, i + 1) for i in range(count - 1)]
        backward = [(target, source) for source, target in forward]
        low = lax.ppermute(
            lax.slice_in_dim(block, block.shape[dim] - width, None, axis=dim), axis, forward
        )
        high = lax.ppermute(lax.slice_in_dim(block, 0, width, axis=dim), axis, backward)
        block = jnp.concatenate([low, block, high], axis=dim)
    return block


def per_device(amplitudes, integrals, cycle_terms, ladder_factors, live):
    local_tiles = amplitudes.shape[0]
    occupied = amplitudes.shape[1]
    band_slots = amplitudes.shape[3]
    tile_size = amplitudes.shape[4]
    factor_count = ladder_factors.shape[1]
    half_band = band_slots // 2
    slot_index = jnp.arange(band_slots)
    global_rows = lax.axis_index("vir") * local_tiles + jnp.arange(local_tiles)
    col_tile = global_rows[:, None] + slot_index[None, :] - half_band
    inside = (col_tile >= 0) & (col_tile < NT)
    keep = ((live == 1) | (slot_index == half_band)[None, None, None, :]) & inside[:, None, None, :]
    keep_float = keep.astype(jnp.float32)[..., None, None]
    amps = amplitudes * keep_float
    pair_tiles = occupied * occupied * band_slots
    joined = jnp.concatenate(
        [cycle_terms.reshape(local_tiles, pair_tiles, tile_size, tile_size), ladder_factors], axis=1
    )
    widened = extended(joined, (("vir", 0),), half_band)
    cycle_ext = widened[:, :pair_tiles].reshape(
        local_tiles + 2 * half_band, occupied, occupied, band_slots, tile_size, tile_size
    )
    factors = widened[:, pair_tiles:]
    cycle_all = lax.all_gather(cycle_ext, "row", axis=1, tiled=True)
    centre = factors[half_band : half_band + local_tiles]
    ladder = jnp.zeros(amplitudes.shape, jnp.float32)
    for term_index in range(factor_count):
        inner = jnp.einsum(
            "axy,aijsyz->aijsxz", centre[:, term_index], amps, precision=lax.Precision.HIGHEST
        )
        parts = []
        for out_slot in range(band_slots):
            right_side = factors[out_slot : out_slot + local_tiles, term_index]
            parts.append(
                jnp.einsum(
                    "aijxz,awz->aijxw",
                    inner[:, :, :, out_slot],
                    right_side,
                    precision=lax.Precision.HIGHEST,
                )
            )
        ladder = ladder + jnp.stack(parts, axis=3)
    piece = lax.all_gather(amps, "col", axis=2, tiled=True)
    slot_sums = []
    for out_slot in range(band_slots):
        summed = jnp.zeros((local_tiles, occupied, occupied, tile_size, tile_size), jnp.float32)
        for in_slot in range(band_slots):
            mid_slot = out_slot - in_slot + half_band
            if 0 <= mid_slot < band_slots:
                cycle_rows = cycle_all[in_slot : in_slot + local_tiles, :, :, mid_slot]
                summed = summed + jnp.einsum(
                    "aiktu,akjuv->aijtv",
                    piece[:, :, :, in_slot],
                    cycle_rows,
                    precision=lax.Precision.HIGHEST,
                )
        slot_sums.append(summed)
    cycle = jnp.stack(slot_sums, axis=3)
    return keep_float * (integrals + ladder + cycle)


def solution(mesh):
    in_specs = (
        P("vir", "row", "col", None, None, None),
        P("vir", "row", "col", None, None, None),
        P("vir", "row", "col", None, None, None),
        P("vir", None, None, None),
        P("vir", "row", "col", None),
    )
    out_specs = P("vir", "row", "col", None, None, None)
    return jax.shard_map(
        per_device, mesh=mesh, in_specs=in_specs, out_specs=out_specs, check_vma=False
    )
```

profile of v0, /device:TPU:0, one launch (start us, length us, event | category | flops | bytes accessed | tf_op | source)
XLA Modules:
  0.0 918.6 jit_solution(8032832479250462117)
XLA Ops:
  27.4 14.0 %collective-permute-done = f32[1,11,128,128]{3,2,0,1:T(8,128)S(1)} collective-permute-done((f32[1,11,128,128]{3,2,0,1:T(8,128)S(1)}, f32[1,11,128,128]{3,2,0,1:T(8,128)S(1)}, u32[]{:S(2)}, u32[]{:S(2)}) %collective-permute-start) | collective-permute-done | bytes 720928 | tf_op jit(solution)/shard_map/ppermute | solution.py:14
  49.9 17.9 %fusion.32 = f32[40,1,1,3,128,128]{4,5,3,0,2,1:T(8,128)S(1)} fusion(f32[40,3]{0,1:T(4,128)S(1)} %bitcast.514, f32[40,1,1,3,128,128]{5,4,3,2,1,0:T(8,128)} %param.5, f32[40,8,128,128]{3,2,1,0:T(8,128)} %param.8), kind=kOutput, calls=%fused_computation.48 | convolution fusion | flops 3021864960 | bytes 18350560 | tf_op jit(solution)/shard_map/axy,aijsyz->aijsxz/dot_general | solution.py:49
  71.0 8.0 fusion.178
  79.1 18.1 %fusion.35 = f32[40,1,1,3,128,128]{4,5,3,0,2,1:T(8,128)} fusion(f32[40,3]{0,1:T(4,128)S(1)} %bitcast.515, f32[40,1,1,3,128,128]{5,4,3,2,1,0:T(8,128)} %param.5, f32[40,8,128,128]{3,2,1,0:T(8,128)} %param.8), kind=kOutput, calls=%fused_computation.49 | convolution fusion | flops 3021864960 | bytes 18350560 | tf_op jit(solution)/shard_map/axy,aijsyz->aijsxz/dot_general | solution.py:49
  104.9 15.8 %fusion.38 = f32[40,1,1,3,128,128]{4,5,3,0,2,1:T(8,128)} fusion(f32[40,3]{0,1:T(4,128)S(1)} %bitcast.516, f32[40,1,1,3,128,128]{5,4,3,2,1,0:T(8,128)S(1)} %bitcast.501, f32[40,8,128,128]{3,2,1,0:T(8,128)S(1)} %bitcast.499), kind=kOutput, calls=%fused_computation.50 | convolution fusion | flops 3021864960 | bytes 18352128 | tf_op jit(solution)/shard_map/axy,aijsyz->aijsxz/dot_general | solution.py:49
  128.3 15.5 %fusion.41 = f32[40,1,1,3,128,128]{4,5,3,0,2,1:T(8,128)} fusion(f32[40,3]{0,1:T(4,128)S(1)} %bitcast.517, f32[40,1,1,3,128,128]{5,4,3,2,1,0:T(8,128)S(1)} %bitcast.501, f32[40,8,128,128]{3,2,1,0:T(8,128)S(1)} %bitcast.499), kind=kOutput, calls=%fused_computation.51 | convolution fusion | flops 3021864960 | bytes 18352128 | tf_op jit(solution)/shard_map/axy,aijsyz->aijsxz/dot_general | solution.py:49
  151.6 15.6 %fusion.44 = f32[40,1,1,3,128,128]{4,5,3,0,2,1:T(8,128)} fusion(f32[40,3]{0,1:T(4,128)S(1)} %bitcast.518, f32[40,1,1,3,128,128]{5,4,3,2,1,0:T(8,128)S(1)} %bitcast.501, f32[40,8,128,128]{3,2,1,0:T(8,128)S(1)} %bitcast.499), kind=kOutput, calls=%fused_computation.52 | convolution fusion | flops 3021864960 | bytes 18352128 | tf_op jit(solution)/shard_map/axy,aijsyz->aijsxz/dot_general | solution.py:49
  174.9 15.9 %fusion.47 = f32[40,1,1,3,128,128]{4,5,3,0,2,1:T(8,128)} fusion(f32[40,3]{0,1:T(4,128)S(1)} %bitcast.519, f32[40,1,1,3,128,128]{5,4,3,2,1,0:T(8,128)S(1)} %bitcast.501, f32[40,8,128,128]{3,2,1,0:T(8,128)S(1)} %bitcast.499), kind=kOutput, calls=%fused_computation.53 | convolution fusion | flops 3021864960 | bytes 18352128 | tf_op jit(solution)/shard_map/axy,aijsyz->aijsxz/dot_general | solution.py:49
  198.5 15.6 %fusion.50 = f32[40,1,1,3,128,128]{4,5,3,0,2,1:T(8,128)} fusion(f32[40,3]{0,1:T(4,128)S(1)} %bitcast.520, f32[40,1,1,3,128,128]{5,4,3,2,1,0:T(8,128)S(1)} %bitcast.501, f32[40,8,128,128]{3,2,1,0:T(8,128)S(1)} %bitcast.499), kind=kOutput, calls=%fused_computation.54 | convolution fusion | flops 3021864960 | bytes 18352128 | tf_op jit(solution)/shard_map/axy,aijsyz->aijsxz/dot_general | solution.py:49
  221.9 18.1 %fusion.53 = f32[40,1,1,3,128,128]{4,5,3,0,2,1:T(8,128)} fusion(f32[40,3]{0,1:T(4,128)S(1)} %bitcast.521, f32[40,1,1,3,128,128]{5,4,3,2,1,0:T(8,128)} %param.5, f32[40,8,128,128]{3,2,1,0:T(8,128)S(1)} %bitcast.499), kind=kOutput, calls=%fused_computation.55 | convolution fusion | flops 3021864960 | bytes 18352128 | tf_op jit(solution)/shard_map/axy,aijsyz->aijsxz/dot_general | solution.py:49
  301.8 8.1 fusion.201
  363.9 8.1 fusion.181
  372.0 173.2 %all-gather.4.cloned.1.call-done = f32[40,1,4,3,128,128]{5,4,3,1,0,2:T(8,128)} async-done(((f32[40,1,1,3,128,128]{5,4,3,1,0,2:T(8,128)}), f32[40,1,4,3,128,128]{5,4,3,1,0,2:T(8,128)}) %all-gather.4.cloned.1.call-update) | async-done | bytes 31457296 | tf_op jit(solution)/shard_map/all_gather | solution.py:64
  545.2 25.9 %fusion.237 = (f32[40,1,4,1,128,128]{5,4,3,1,0,2:T(8,128)}, f32[40,1,4,1,128,128]{5,4,3,1,0,2:T(8,128)}, f32[40,1,4,1,128,128]{5,4,3,1,0,2:T(8,128)}) fusion(f32[40,1,4,3,128,128]{5,4,3,1,0,2:T(8,128)} %all-gather.4.cloned.1.call-done), kind=kLoop, calls=%fused_computation.267 | loop fusion | bytes 62914560 | tf_op jit(solution)/shard_map/slice | solution.py:74
  571.1 172.4 %all-gather.6.cloned.1.call-done = f32[42,12,128,128]{3,2,0,1:T(8,128)} async-done(((f32[42,3,128,128]{3,2,0,1:T(8,128)}), f32[42,12,128,128]{3,2,0,1:T(8,128)}) %all-gather.6.cloned.1.call-update) | async-done | bytes 33030160 | tf_op jit(solution)/shard_map/all_gather | solution.py:45
  743.6 24.3 %copy.172 = f32[42,12,128,128]{3,2,1,0:T(8,128)} copy(f32[42,12,128,128]{3,2,0,1:T(8,128)} %all-gather.6.cloned.1.call-done) | data formatting | bytes 66060288 | tf_op jit(solution)/shard_map/all_gather | solution.py:45
  768.2 15.4 %fusion.4 = f32[40,128,128,1]{1,2,3,0:T(8,128)} fusion(f32[42,4,1,3,128,128]{5,4,3,1,0,2:T(8,128)} %bitcast.502, f32[40,1,4,1,128,128]{5,4,3,1,0,2:T(8,128)S(1)} %copy-done.1), kind=kOutput, calls=%fused_computation.9 | convolution fusion | flops 4026531840 | bytes 23592960 | tf_op jit(solution)/shard_map/aiktu,akjuv->aijtv/dot_general | solution.py:72
  783.6 16.2 %fusion.6 = f32[40,128,128,1]{1,2,3,0:T(8,128)S(1)} fusion(f32[42,4,1,3,128,128]{5,4,3,1,0,2:T(8,128)} %bitcast.503, f32[40,1,4,1,128,128]{5,4,3,1,0,2:T(8,128)} %get-tuple-element.5), kind=kOutput, calls=%fused_computation.13 | convolution fusion | flops 4026531840 | bytes 23592960 | tf_op jit(solution)/shard_map/aiktu,akjuv->aijtv/dot_general | solution.py:72
  799.9 15.3 %fusion.3 = f32[40,128,128,1]{1,2,3,0:T(8,128)} fusion(f32[42,4,1,3,128,128]{5,4,3,1,0,2:T(8,128)} %bitcast.504, f32[40,1,4,1,128,128]{5,4,3,1,0,2:T(8,128)S(1)} %bitcast.510), kind=kOutput, calls=%fused_computation.7 | convolution fusion | flops 4026531840 | bytes 23592960 | tf_op jit(solution)/shard_map/aiktu,akjuv->aijtv/dot_general | solution.py:72
  815.2 15.4 %fusion.1 = f32[40,128,128,1]{1,2,3,0:T(8,128)} fusion(f32[42,4,1,3,128,128]{5,4,3,1,0,2:T(8,128)} %bitcast.505, f32[40,1,4,1,128,128]{5,4,3,1,0,2:T(8,128)S(1)} %bitcast.510), kind=kOutput, calls=%fused_computation.3 | convolution fusion | flops 4026531840 | bytes 23592960 | tf_op jit(solution)/shard_map/aiktu,akjuv->aijtv/dot_general | solution.py:72
  830.6 15.6 %fusion.152 = f32[40,1,1,1,128,128]{5,4,0,3,2,1:T(8,128)} fusion(f32[40,128,128,1]{1,2,3,0:T(8,128)S(1)} %fusion.6, f32[40,1,4,1,128,128]{5,4,3,1,0,2:T(8,128)S(1)} %bitcast.510, f32[42,4,1,3,128,128]{5,4,3,1,0,2:T(8,128)} %bitcast.506), kind=kOutput, calls=%fused_computation.196 | convolution fusion | flops 4027187200 | bytes 26214400 | tf_op jit(solution)/shard_map/aiktu,akjuv->aijtv/dot_general | solution.py:72
  846.2 20.5 %fusion.150 = f32[40,1,1,1,128,128]{5,4,0,3,2,1:T(8,128)} fusion(f32[40,128,128,1]{1,2,3,0:T(8,128)} %fusion.1, f32[40,1,4,1,128,128]{5,4,3,1,0,2:T(8,128)} %get-tuple-element.7, f32[42,4,1,3,128,128]{5,4,3,1,0,2:T(8,128)} %bitcast.507), kind=kOutput, calls=%fused_computation.191 | convolution fusion | flops 4027187200 | bytes 26214400 | tf_op jit(solution)/shard_map/aiktu,akjuv->aijtv/dot_general | solution.py:72
  866.7 16.1 %fusion.151 = f32[40,1,1,1,128,128]{5,4,0,3,2,1:T(8,128)} fusion(f32[40,128,128,1]{1,2,3,0:T(8,128)} %fusion.3, f32[40,128,128,1]{1,2,3,0:T(8,128)S(1)} %copy-done.4, f32[40,1,4,1,128,128]{5,4,3,1,0,2:T(8,128)S(1)} %bitcast.512, f32[42,4,1,3,128,128]{5,4,3,1,0,2:T(8,128)} %bitcast.508), kind=kOutput, calls=%fused_computation.193 | convolution fusion | flops 4027842560 | bytes 28835840 | tf_op jit(solution)/shard_map/aiktu,akjuv->aijtv/dot_general | solution.py:72
  882.9 25.0 %fusion.15 = f32[40,1,1,3,128,128]{5,4,0,3,2,1:T(8,128)S(1)} fusion(f32[40,1,1,1,128,128]{5,4,0,3,2,1:T(8,128)} %fusion.181, f32[40,1,1,1,128,128]{5,4,0,3,2,1:T(8,128)} %fusion.178, f32[40,1,1,1,128,128]{5,4,0,3,2,1:T(8,128)} %fusion.177, f32[40,1,1,1,128,128]{5,4,0,3,2,1:T(8,128)} %fusion.186, f32[40,1,1,1,128,128]{5,4,0,3,2,1:T(8,128)} %fusion.183, ...), kind=kLoop, calls=%fused_computation.29 | loop fusion | flops 55050240 | bytes 86508000 | tf_op jit(solution)/shard_map/mul | solution.py:80
  (87 shorter events, 198.8 us)
Async XLA Ops:
  6.5 538.7 %all-gather.4.cloned.1.call-start = ((), (), s32[]{:S(2)}) async-start(), calls=%async_computation | async-start | bytes 39321600 | tf_op jit(solution)/shard_map/all_gather | solution.py:64
  7.3 214.6 %copy-start.5 = (f32[40,1,1,3]{0,3,2,1:T(4,128)}, f32[40,1,1,3]{0,3,2,1:T(4,128)S(1)}, u32[]{:S(2)}) copy-start(f32[40,1,1,3]{0,3,2,1:T(4,128)S(1)} %copy.436) | copy-start | bytes 1444
  15.3 728.3 %all-gather.6.cloned.1.call-start = ((), (), s32[]{:S(2)}) async-start(), calls=%async_computation.1 | async-start | bytes 41287680 | tf_op jit(solution)/shard_map/all_gather | solution.py:45
  19.1 26.5 %copy-start = (f32[40,1,1,3,128,128]{5,4,0,3,2,1:T(8,128)}, f32[40,1,1,3,128,128]{5,4,0,3,2,1:T(8,128)S(1)}, u32[]{:S(2)}) copy-start(f32[40,1,1,3,128,128]{5,4,0,3,2,1:T(8,128)S(1)} %copy.435) | copy-start | bytes 23592964
  21.2 20.3 %collective-permute-start = (f32[1,11,128,128]{3,2,0,1:T(8,128)S(1)}, f32[1,11,128,128]{3,2,0,1:T(8,128)S(1)}, u32[]{:S(2)}, u32[]{:S(2)}) collective-permute-start(f32[1,11,128,128]{3,2,0,1:T(8,128)S(1)} %get-tuple-element.8), channel_id=1, source_target_pairs={{0,1},{2,3},{4,5},{6,7},{8,9},{10,11},{12,13},{14,15},{16,17},{18,... | collective-permute-start | bytes 2162696 | tf_op jit(solution)/shard_map/ppermute | solution.py:14
  26.1 19.5 %collective-permute-start.1 = (f32[1,11,128,128]{3,2,0,1:T(8,128)S(1)}, f32[1,11,128,128]{3,2,0,1:T(8,128)S(1)}, u32[]{:S(2)}, u32[]{:S(2)}) collective-permute-start(f32[1,11,128,128]{3,2,0,1:T(8,128)S(1)} %get-tuple-element.9), channel_id=1, source_target_pairs={{1,0},{3,2},{5,4},{7,6},{9,8},{11,10},{13,12},{15,14},{17,16},{19,... | collective-permute-start | bytes 2162696 | tf_op jit(solution)/shard_map/ppermute | solution.py:17
  49.9 47.3 %slice-start.2 = ((s8[20971520]{0:T(1024)(128)(4,1)}), s8[4194304]{0:T(1024)(128)(4,1)S(1)}, s32[]{:S(2)}) async-start(s8[20971520]{0:T(1024)(128)(4,1)} %bitcast.498), calls=%async_computation.4 | async-start | bytes 8388608
  49.9 47.3 %slice-start.3 = ((s8[20971520]{0:T(1024)(128)(4,1)}), s8[4194304]{0:T(1024)(128)(4,1)S(1)}, s32[]{:S(2)}) async-start(s8[20971520]{0:T(1024)(128)(4,1)} %bitcast.498), calls=%async_computation.5 | async-start | bytes 8388608
  49.9 47.3 %slice-start.4 = ((s8[20971520]{0:T(1024)(128)(4,1)}), s8[4194304]{0:T(1024)(128)(4,1)S(1)}, s32[]{:S(2)}) async-start(s8[20971520]{0:T(1024)(128)(4,1)} %bitcast.498), calls=%async_computation.6 | async-start | bytes 8388608
  71.0 33.9 %slice-start.7 = ((s8[7864320]{0:T(1024)(128)(4,1)}), s8[4194304]{0:T(1024)(128)(4,1)S(1)}, s32[]{:S(2)}) async-start(s8[7864320]{0:T(1024)(128)(4,1)} %bitcast.500), calls=%async_computation.9 | async-start | bytes 8388608
  79.1 18.1 %slice-start.5 = ((s8[20971520]{0:T(1024)(128)(4,1)}), s8[4194304]{0:T(1024)(128)(4,1)S(1)}, s32[]{:S(2)}) async-start(s8[20971520]{0:T(1024)(128)(4,1)} %bitcast.498), calls=%async_computation.7 | async-start | bytes 8388608
  79.1 18.2 %slice-start.6 = ((s8[20971520]{0:T(1024)(128)(4,1)}), s8[4194304]{0:T(1024)(128)(4,1)S(1)}, s32[]{:S(2)}) async-start(s8[20971520]{0:T(1024)(128)(4,1)} %bitcast.498), calls=%async_computation.8 | async-start | bytes 8388608
  79.1 25.8 %slice-start.8 = ((s8[7864320]{0:T(1024)(128)(4,1)}), s8[3670016]{0:T(1024)(128)(4,1)S(1)}, s32[]{:S(2)}) async-start(s8[7864320]{0:T(1024)(128)(4,1)} %bitcast.500), calls=%async_computation.10 | async-start | bytes 7340032
  214.0 33.6 %slice-start = ((s8[7864320]{0:T(1024)(128)(4,1)}), s8[4194304]{0:T(1024)(128)(4,1)S(1)}, s32[]{:S(2)}) async-start(s8[7864320]{0:T(1024)(128)(4,1)} %bitcast.480), calls=%async_computation.2 | async-start | bytes 8388608
  221.9 25.7 %slice-start.1 = ((s8[7864320]{0:T(1024)(128)(4,1)}), s8[3670016]{0:T(1024)(128)(4,1)S(1)}, s32[]{:S(2)}) async-start(s8[7864320]{0:T(1024)(128)(4,1)} %bitcast.480), calls=%async_computation.3 | async-start | bytes 7340032
  743.6 24.7 %copy-start.1 = (f32[40,1,4,1,128,128]{5,4,3,1,0,2:T(8,128)S(1)}, f32[40,1,4,1,128,128]{5,4,3,1,0,2:T(8,128)}, u32[]{:S(2)}) copy-start(f32[40,1,4,1,128,128]{5,4,3,1,0,2:T(8,128)} %get-tuple-element.5) | copy-start | bytes 31457284
  768.2 31.7 %slice-start.9 = ((s8[10485760]{0:T(1024)(128)(4,1)}), s8[4194304]{0:T(1024)(128)(4,1)S(1)}, s32[]{:S(2)}) async-start(s8[10485760]{0:T(1024)(128)(4,1)} %bitcast.509), calls=%async_computation.11 | async-start | bytes 8388608
  768.2 31.7 %slice-start.10 = ((s8[10485760]{0:T(1024)(128)(4,1)}), s8[4194304]{0:T(1024)(128)(4,1)S(1)}, s32[]{:S(2)}) async-start(s8[10485760]{0:T(1024)(128)(4,1)} %bitcast.509), calls=%async_computation.12 | async-start | bytes 8388608
  783.6 16.3 %slice-start.11 = ((s8[10485760]{0:T(1024)(128)(4,1)}), s8[2097152]{0:T(1024)(128)(4,1)S(1)}, s32[]{:S(2)}) async-start(s8[10485760]{0:T(1024)(128)(4,1)} %bitcast.509), calls=%async_computation.13 | async-start | bytes 4194304
  830.6 36.1 %slice-start.12 = ((s8[10485760]{0:T(1024)(128)(4,1)}), s8[2097152]{0:T(1024)(128)(4,1)S(1)}, s32[]{:S(2)}) async-start(s8[10485760]{0:T(1024)(128)(4,1)} %bitcast.511), calls=%async_computation.14 | async-start | bytes 4194304
  830.6 36.1 %slice-start.13 = ((s8[10485760]{0:T(1024)(128)(4,1)}), s8[4194304]{0:T(1024)(128)(4,1)S(1)}, s32[]{:S(2)}) async-start(s8[10485760]{0:T(1024)(128)(4,1)} %bitcast.511), calls=%async_computation.15 | async-start | bytes 8388608
  846.2 20.5 %slice-start.14 = ((s8[10485760]{0:T(1024)(128)(4,1)}), s8[4194304]{0:T(1024)(128)(4,1)S(1)}, s32[]{:S(2)}) async-start(s8[10485760]{0:T(1024)(128)(4,1)} %bitcast.511), calls=%async_computation.16 | async-start | bytes 8388608
  846.2 20.5 %copy-start.4 = (f32[40,128,128,1]{1,2,3,0:T(8,128)S(1)}, f32[40,128,128,1]{1,2,3,0:T(8,128)}, u32[]{:S(2)}) copy-start(f32[40,128,128,1]{1,2,3,0:T(8,128)} %fusion.4) | copy-start | bytes 7864324
  866.7 16.2 %copy-start.3 = (f32[40,1,1,1,128,128]{5,4,0,3,2,1:T(8,128)S(1)}, f32[40,1,1,1,128,128]{5,4,0,3,2,1:T(8,128)}, u32[]{:S(2)}) copy-start(f32[40,1,1,1,128,128]{5,4,0,3,2,1:T(8,128)} %fusion.182) | copy-start | bytes 7864324
  (2 other events, 19.4 us)
Sparse Core Ops, SparseCore 0:
  15.4 529.8 all-gather.3
  546.8 196.6 all-gather.5
where the time goes:
time: 922 us; the launch traced here: 919 us
  matrix products  433 us (47%)
  waiting for transfers between devices  364 us (39%)
  local copies, waits for them, and re-layouts  65.5 us (7%)
  other arithmetic  35.8 us (4%)
  between operations  13.8 us (1%)
    dot_general x24, matrix products, per_device(): jnp.einsum('aijxz,awz->aijxw', inner[:, :, :, out_slot], right_side, prec...  186 us
    all_gather x1, waiting for transfers between devices, per_device(): piece = lax.all_gather(amps, 'col', axis=2, tiled=True)  173 us
    all_gather x1, waiting for transfers between devices, per_device(): cycle_all = lax.all_gather(cycle_ext, 'row', axis=1, tiled=True)  172 us
    dot_general x8, matrix products, per_device(): jnp.einsum('axy,aijsyz->aijsxz', centre[:, term_index], amps, precision=l...  132 us
    dot_general x7, matrix products, per_device(): jnp.einsum('aiktu,akjuv->aijtv', piece[:, :, :, in_slot], cycle_rows, pre...  115 us
    slice x1, local copies, waits for them, and re-layouts, per_device(): piece[:, :, :, in_slot]  25.9 us
    mul x2, other arithmetic, per_device(): return keep_float * (integrals + ladder + cycle)  25.7 us
    all_gather x1, local copies, waits for them, and re-layouts, per_device(): cycle_all = lax.all_gather(cycle_ext, 'row', axis=1, tiled=True)  24.3 us
  transfers between devices with their start and end apart: 4, of which 4 were waited for; matrix products, arithmetic and copies ran while one was open for 39% of the time, Pallas kernels for 0%

commit v1 on v0

--- a/solution.py
+++ b/solution.py
@@ -42,7 +42,26 @@
         local_tiles + 2 * half_band, occupied, occupied, band_slots, tile_size, tile_size
     )
     factors = widened[:, pair_tiles:]
-    cycle_all = lax.all_gather(cycle_ext, "row", axis=1, tiled=True)
+    size, position, rows = (lax.axis_size("row"), lax.axis_index("row"), cycle_ext.shape[1])
+    ahead = [(i_2, (i_2 + 1) % size) for i_2 in range(size)]
+    left = [(i_2, (i_2 - 1) % size) for i_2 in range(size)]
+    whole = jnp.zeros(
+        (*cycle_ext.shape[:1], size * rows, *cycle_ext.shape[1 + 1 :]), cycle_ext.dtype
+    )
+    whole = lax.dynamic_update_slice_in_dim(whole, cycle_ext, position * rows, axis=1)
+    from_left = from_right = cycle_ext
+    half = size // 2
+    for step in range(1, half + 1):
+        from_left = lax.ppermute(from_left, "row", ahead)
+        whole = lax.dynamic_update_slice_in_dim(
+            whole, from_left, (position - step) % size * rows, axis=1
+        )
+        if step < size - half:
+            from_right = lax.ppermute(from_right, "row", left)
+            whole = lax.dynamic_update_slice_in_dim(
+                whole, from_right, (position + step) % size * rows, axis=1
+            )
+    cycle_all = whole
     centre = factors[half_band : half_band + local_tiles]
     ladder = jnp.zeros(amplitudes.shape, jnp.float32)
     for term_index in range(factor_count):

time: 922 us -> 713 us (0.77)
  waiting for transfers between devices: 364 us -> 113 us
  local copies, waits for them, and re-layouts: 65.5 us -> 112 us
    all_gather x1 -> x0, waiting for transfers between devices: 172 us -> none  [per_device(): cycle_all = lax.all_gather(cycle_ext, 'row', axis=1, tiled=True)]
    all_gather x1, waiting for transfers between devices: 173 us -> 94.6 us  [per_device(): piece = lax.all_gather(amps, 'col', axis=2, tiled=True)]
    dynamic_update_slice x0 -> x4, local copies, waits for them, and re-layouts: none -> 27.5 us  [the longest x2 15.4 us: per_device(): lax.dynamic_update_slice_in_dim(whole, from_left, (position - step) % siz...]
    ppermute x0 -> x3, local copies, waits for them, and re-layouts: none -> 26.7 us  [the longest x2 17.7 us: per_device(): from_left = lax.ppermute(from_left, 'row', ahead)]
    all_gather x1 -> x0, local copies, waits for them, and re-layouts: 24.3 us -> none  [per_device(): cycle_all = lax.all_gather(cycle_ext, 'row', axis=1, tiled=True)]
    broadcast_in_dim x0 -> x1, local copies, waits for them, and re-layouts: none -> 16.7 us  [per_device(): jnp.zeros((*cycle_ext.shape[:1], size * rows, *cycle_ext.shape[1 + 1:]),...]
  transfers between devices with their start and end apart: 4 -> 6, of which waited for: 4 -> 3; matrix products, arithmetic and copies ran while one was open for 39% -> 57% of each run, Pallas kernels for 0% -> 0%
where the time goes in v1:
time: 713 us; the launch traced here: 709 us
  matrix products  425 us (60%)
  waiting for transfers between devices  113 us (16%)
  local copies, waits for them, and re-layouts  112 us (16%)
  other arithmetic  35.6 us (5%)
  between operations  14.2 us (2%)
  starting transfers between devices  8.55 us (1%)
    dot_general x24, matrix products, per_device(): jnp.einsum('aijxz,awz->aijxw', inner[:, :, :, out_slot], right_side, prec...  186 us
    dot_general x8, matrix products, per_device(): jnp.einsum('axy,aijsyz->aijsxz', centre[:, term_index], amps, precision=l...  130 us
    dot_general x7, matrix products, per_device(): jnp.einsum('aiktu,akjuv->aijtv', piece[:, :, :, in_slot], cycle_rows, pre...  110 us
    all_gather x1, waiting for transfers between devices, per_device(): piece = lax.all_gather(amps, 'col', axis=2, tiled=True)  94.6 us
    mul x2, other arithmetic, per_device(): return keep_float * (integrals + ladder + cycle)  25.9 us
    ppermute x2, local copies, waits for them, and re-layouts, per_device(): from_left = lax.ppermute(from_left, 'row', ahead)  17.7 us
    slice x1, local copies, waits for them, and re-layouts, per_device(): piece[:, :, :, in_slot]  17.7 us
    broadcast_in_dim x1, local copies, waits for them, and re-layouts, per_device(): jnp.zeros((*cycle_ext.shape[:1], size * rows, *cycle_ext.shape[1 + 1:]),...  16.7 us
  transfers between devices with their start and end apart: 6, of which 3 were waited for; matrix products, arithmetic and copies ran while one was open for 57% of the time, Pallas kernels for 0%

profile of v1, /device:TPU:0, one launch (start us, length us, event | category | flops | bytes accessed | tf_op | source)
XLA Modules:
  0.0 708.9 jit_solution(1353809689329687328)
XLA Ops:
  27.4 14.0 %collective-permute-done = f32[1,11,128,128]{3,2,0,1:T(8,128)S(1)} collective-permute-done((f32[1,11,128,128]{3,2,0,1:T(8,128)S(1)}, f32[1,11,128,128]{3,2,0,1:T(8,128)S(1)}, u32[]{:S(2)}, u32[]{:S(2)}) %collective-permute-start) | collective-permute-done | bytes 720928 | tf_op jit(solution)/shard_map/ppermute | solution.py:14
  49.9 17.8 %fusion.33 = f32[40,1,1,3,128,128]{4,5,3,0,2,1:T(8,128)S(1)} fusion(f32[40,3]{0,1:T(4,128)S(1)} %bitcast.501, f32[40,1,1,3,128,128]{5,4,3,2,1,0:T(8,128)} %param.5, f32[40,8,128,128]{3,2,1,0:T(8,128)} %param.8), kind=kOutput, calls=%fused_computation.49 | convolution fusion | flops 3021864960 | bytes 18350560 | tf_op jit(solution)/shard_map/axy,aijsyz->aijsxz/dot_general | solution.py:68
  78.7 18.0 %fusion.36 = f32[40,1,1,3,128,128]{4,5,3,0,2,1:T(8,128)} fusion(f32[40,3]{0,1:T(4,128)S(1)} %bitcast.502, f32[40,1,1,3,128,128]{5,4,3,2,1,0:T(8,128)} %param.5, f32[40,8,128,128]{3,2,1,0:T(8,128)} %param.8), kind=kOutput, calls=%fused_computation.50 | convolution fusion | flops 3021864960 | bytes 18350560 | tf_op jit(solution)/shard_map/axy,aijsyz->aijsxz/dot_general | solution.py:68
  104.5 15.8 %fusion.39 = f32[40,1,1,3,128,128]{4,5,3,0,2,1:T(8,128)} fusion(f32[40,3]{0,1:T(4,128)S(1)} %bitcast.503, f32[40,1,1,3,128,128]{5,4,3,2,1,0:T(8,128)S(1)} %bitcast.497, f32[40,8,128,128]{3,2,1,0:T(8,128)S(1)} %bitcast.493), kind=kOutput, calls=%fused_computation.51 | convolution fusion | flops 3021864960 | bytes 18352128 | tf_op jit(solution)/shard_map/axy,aijsyz->aijsxz/dot_general | solution.py:68
  128.0 15.6 %fusion.42 = f32[40,1,1,3,128,128]{4,5,3,0,2,1:T(8,128)} fusion(f32[40,3]{0,1:T(4,128)S(1)} %bitcast.504, f32[40,1,1,3,128,128]{5,4,3,2,1,0:T(8,128)S(1)} %bitcast.497, f32[40,8,128,128]{3,2,1,0:T(8,128)S(1)} %bitcast.493), kind=kOutput, calls=%fused_computation.52 | convolution fusion | flops 3021864960 | bytes 18352128 | tf_op jit(solution)/shard_map/axy,aijsyz->aijsxz/dot_general | solution.py:68
  151.3 15.6 %fusion.45 = f32[40,1,1,3,128,128]{4,5,3,0,2,1:T(8,128)} fusion(f32[40,3]{0,1:T(4,128)S(1)} %bitcast.505, f32[40,1,1,3,128,128]{5,4,3,2,1,0:T(8,128)S(1)} %bitcast.497, f32[40,8,128,128]{3,2,1,0:T(8,128)S(1)} %bitcast.493), kind=kOutput, calls=%fused_computation.53 | convolution fusion | flops 3021864960 | bytes 18352128 | tf_op jit(solution)/shard_map/axy,aijsyz->aijsxz/dot_general | solution.py:68
  174.5 15.6 %fusion.48 = f32[40,1,1,3,128,128]{4,5,3,0,2,1:T(8,128)} fusion(f32[40,3]{0,1:T(4,128)S(1)} %bitcast.506, f32[40,1,1,3,128,128]{5,4,3,2,1,0:T(8,128)S(1)} %bitcast.497, f32[40,8,128,128]{3,2,1,0:T(8,128)S(1)} %bitcast.493), kind=kOutput, calls=%fused_computation.54 | convolution fusion | flops 3021864960 | bytes 18352128 | tf_op jit(solution)/shard_map/axy,aijsyz->aijsxz/dot_general | solution.py:68
  191.8 15.8 %fusion.51 = f32[40,1,1,3,128,128]{4,5,3,0,2,1:T(8,128)} fusion(f32[40,3]{0,1:T(4,128)S(1)} %bitcast.507, f32[40,1,1,3,128,128]{5,4,3,2,1,0:T(8,128)S(1)} %bitcast.497, f32[40,8,128,128]{3,2,1,0:T(8,128)S(1)} %bitcast.493), kind=kOutput, calls=%fused_computation.55 | convolution fusion | flops 3021864960 | bytes 18352128 | tf_op jit(solution)/shard_map/axy,aijsyz->aijsxz/dot_general | solution.py:68
  223.1 15.7 %fusion.54 = f32[40,1,1,3,128,128]{4,5,3,0,2,1:T(8,128)} fusion(f32[40,3]{0,1:T(4,128)S(1)} %bitcast.508, f32[40,1,1,3,128,128]{5,4,3,2,1,0:T(8,128)S(1)} %bitcast.497, f32[40,8,128,128]{3,2,1,0:T(8,128)S(1)} %bitcast.493), kind=kOutput, calls=%fused_computation.56 | convolution fusion | flops 3021864960 | bytes 18352128 | tf_op jit(solution)/shard_map/axy,aijsyz->aijsxz/dot_general | solution.py:68
  246.6 8.9 %copy.113 = f32[42,1,1,3,128,128]{4,5,1,0,3,2:T(8,128)} copy(f32[42,1,1,3,128,128]{5,4,0,3,2,1:T(8,128)} %fusion.7) | data formatting | bytes 16515072 | tf_op jit(solution)/shard_map/reshape | solution.py:41
  255.5 16.7 %broadcast_in_dim.2 = f32[42,4,1,3,128,128]{4,5,1,0,3,2:T(8,128)} broadcast(f32[]{:T(128)} %constant.44.clone.1), dimensions={} | broadcast | bytes 33030148 | tf_op jit(solution)/shard_map/broadcast_in_dim | solution.py:48
  404.2 8.9 %copy.114 = f32[42,1,1,3,128,128]{4,5,1,0,3,2:T(8,128)} copy(f32[42,1,1,3,128,128]{5,4,0,3,2,1:T(8,128)} %collective-permute-done.2) | data formatting | bytes 16515072 | tf_op jit(solution)/shard_map/ppermute | solution.py:55
  413.1 9.0 %copy.115 = f32[42,1,1,3,128,128]{4,5,1,0,3,2:T(8,128)} copy(f32[42,1,1,3,128,128]{5,4,0,3,2,1:T(8,128)} %collective-permute-done.3) | data formatting | bytes 16515072 | tf_op jit(solution)/shard_map/ppermute | solution.py:60
  434.0 8.9 %copy.116 = f32[42,1,1,3,128,128]{4,5,1,0,3,2:T(8,128)} copy(f32[42,1,1,3,128,128]{5,4,0,3,2,1:T(8,128)} %collective-permute-done.4) | data formatting | bytes 16515072 | tf_op jit(solution)/shard_map/ppermute | solution.py:55
  450.6 94.6 %all-gather.2.cloned.1.call-done = f32[40,1,4,3,128,128]{5,4,3,1,0,2:T(8,128)} async-done(((f32[40,1,1,3,128,128]{5,4,3,1,0,2:T(8,128)}), f32[40,1,4,3,128,128]{5,4,3,1,0,2:T(8,128)}) %all-gather.2.cloned.1.call-update) | async-done | bytes 31457296 | tf_op jit(solution)/shard_map/all_gather | solution.py:83
  545.2 17.7 %fusion.238 = (f32[40,1,4,1,128,128]{5,4,3,1,0,2:T(8,128)}, f32[40,1,4,1,128,128]{5,4,3,1,0,2:T(8,128)S(1)}, f32[40,1,4,1,128,128]{5,4,3,1,0,2:T(8,128)}) fusion(f32[40,1,4,3,128,128]{5,4,3,1,0,2:T(8,128)} %all-gather.2.cloned.1.call-done), kind=kLoop, calls=%fused_computation.272 | loop fusion | bytes 62914560 | tf_op jit(solution)/shard_map/slice | solution.py:93
  562.9 14.6 %fusion.6 = f32[40,128,128,1]{1,2,3,0:T(8,128)S(1)} fusion(f32[42,4,1,3,128,128]{4,5,1,0,3,2:T(8,128)} %constant_dynamic-update-slice_fusion, f32[40,1,4,1,128,128]{5,4,3,1,0,2:T(8,128)} %get-tuple-element.5), kind=kOutput, calls=%fused_computation.13 | convolution fusion | flops 4026531840 | bytes 23592960 | tf_op jit(solution)/shard_map/aiktu,akjuv->aijtv/dot_general | solution.py:91
  577.5 16.4 %fusion.4 = f32[40,128,128,1]{1,2,3,0:T(8,128)} fusion(f32[42,4,1,3,128,128]{4,5,1,0,3,2:T(8,128)} %constant_dynamic-update-slice_fusion, f32[40,1,4,1,128,128]{5,4,3,1,0,2:T(8,128)} %get-tuple-element.5), kind=kOutput, calls=%fused_computation.9 | convolution fusion | flops 4026531840 | bytes 23592960 | tf_op jit(solution)/shard_map/aiktu,akjuv->aijtv/dot_general | solution.py:91
  593.9 14.5 %fusion.3 = f32[40,128,128,1]{1,2,3,0:T(8,128)} fusion(f32[42,4,1,3,128,128]{4,5,1,0,3,2:T(8,128)} %constant_dynamic-update-slice_fusion, f32[40,1,4,1,128,128]{5,4,3,1,0,2:T(8,128)S(1)} %get-tuple-element.6), kind=kOutput, calls=%fused_computation.7 | convolution fusion | flops 4026531840 | bytes 23592960 | tf_op jit(solution)/shard_map/aiktu,akjuv->aijtv/dot_general | solution.py:91
  608.5 14.6 %fusion.1 = f32[40,128,128,1]{1,2,3,0:T(8,128)} fusion(f32[42,4,1,3,128,128]{4,5,1,0,3,2:T(8,128)} %constant_dynamic-update-slice_fusion, f32[40,1,4,1,128,128]{5,4,3,1,0,2:T(8,128)S(1)} %get-tuple-element.6), kind=kOutput, calls=%fused_computation.3 | convolution fusion | flops 4026531840 | bytes 23592960 | tf_op jit(solution)/shard_map/aiktu,akjuv->aijtv/dot_general | solution.py:91
  623.1 14.7 %fusion.153 = f32[40,1,1,1,128,128]{5,4,0,3,2,1:T(8,128)} fusion(f32[40,128,128,1]{1,2,3,0:T(8,128)S(1)} %fusion.6, f32[40,1,4,1,128,128]{5,4,3,1,0,2:T(8,128)S(1)} %get-tuple-element.6, f32[42,4,1,3,128,128]{4,5,1,0,3,2:T(8,128)} %constant_dynamic-update-slice_fusion), kind=kOutput, calls=%fused_computation.197 | convolution fusion | flops 4027187200 | bytes 26214400 | tf_op jit(solution)/shard_map/aiktu,akjuv->aijtv/dot_general | solution.py:91
  637.8 19.4 %fusion.151 = f32[40,1,1,1,128,128]{5,4,0,3,2,1:T(8,128)} fusion(f32[40,128,128,1]{1,2,3,0:T(8,128)} %fusion.1, f32[40,1,4,1,128,128]{5,4,3,1,0,2:T(8,128)} %get-tuple-element.7, f32[42,4,1,3,128,128]{4,5,1,0,3,2:T(8,128)} %constant_dynamic-update-slice_fusion), kind=kOutput, calls=%fused_computation.192 | convolution fusion | flops 4027187200 | bytes 26214400 | tf_op jit(solution)/shard_map/aiktu,akjuv->aijtv/dot_general | solution.py:91
  657.3 15.3 %fusion.152 = f32[40,1,1,1,128,128]{5,4,0,3,2,1:T(8,128)} fusion(f32[40,128,128,1]{1,2,3,0:T(8,128)} %fusion.3, f32[40,128,128,1]{1,2,3,0:T(8,128)S(1)} %copy-done.4, f32[40,1,4,1,128,128]{5,4,3,1,0,2:T(8,128)S(1)} %bitcast.499, f32[42,4,1,3,128,128]{4,5,1,0,3,2:T(8,128)} %constant_dynamic-update-slice_fusion), kind=kOutput, calls=%fused_computation.194 | convolution fusion | flops 4027842560 | bytes 28835840 | tf_op jit(solution)/shard_map/aiktu,akjuv->aijtv/dot_general | solution.py:91
  672.6 25.2 %fusion.16 = f32[40,1,1,3,128,128]{5,4,0,3,2,1:T(8,128)S(1)} fusion(f32[40,1,1,1,128,128]{5,4,0,3,2,1:T(8,128)} %fusion.182, f32[40,1,1,1,128,128]{5,4,0,3,2,1:T(8,128)} %fusion.179, f32[40,1,1,1,128,128]{5,4,0,3,2,1:T(8,128)} %fusion.178, f32[40,1,1,1,128,128]{5,4,0,3,2,1:T(8,128)} %fusion.187, f32[40,1,1,1,128,128]{5,4,0,3,2,1:T(8,128)} %fusion.184, ...), kind=kLoop, calls=%fused_computation.30 | loop fusion | flops 55050240 | bytes 86508000 | tf_op jit(solution)/shard_map/mul | solution.py:99
  (102 shorter events, 251.2 us)
Async XLA Ops:
  6.5 538.7 %all-gather.2.cloned.1.call-start = ((), (), s32[]{:S(2)}) async-start(), calls=%async_computation | async-start | bytes 39321600 | tf_op jit(solution)/shard_map/all_gather | solution.py:83
  7.3 215.8 %copy-start.5 = (f32[40,1,1,3]{0,3,2,1:T(4,128)}, f32[40,1,1,3]{0,3,2,1:T(4,128)S(1)}, u32[]{:S(2)}) copy-start(f32[40,1,1,3]{0,3,2,1:T(4,128)S(1)} %copy.366) | copy-start | bytes 1444
  19.0 26.5 %copy-start = (f32[40,1,1,3,128,128]{5,4,0,3,2,1:T(8,128)}, f32[40,1,1,3,128,128]{5,4,0,3,2,1:T(8,128)S(1)}, u32[]{:S(2)}) copy-start(f32[40,1,1,3,128,128]{5,4,0,3,2,1:T(8,128)S(1)} %copy.365) | copy-start | bytes 23592964
  21.1 20.3 %collective-permute-start = (f32[1,11,128,128]{3,2,0,1:T(8,128)S(1)}, f32[1,11,128,128]{3,2,0,1:T(8,128)S(1)}, u32[]{:S(2)}, u32[]{:S(2)}) collective-permute-start(f32[1,11,128,128]{3,2,0,1:T(8,128)S(1)} %get-tuple-element.8), channel_id=1, source_target_pairs={{0,1},{2,3},{4,5},{6,7},{8,9},{10,11},{12,13},{14,15},{16,17},{18,... | collective-permute-start | bytes 2162696 | tf_op jit(solution)/shard_map/ppermute | solution.py:14
  26.1 19.5 %collective-permute-start.1 = (f32[1,11,128,128]{3,2,0,1:T(8,128)S(1)}, f32[1,11,128,128]{3,2,0,1:T(8,128)S(1)}, u32[]{:S(2)}, u32[]{:S(2)}) collective-permute-start(f32[1,11,128,128]{3,2,0,1:T(8,128)S(1)} %get-tuple-element.9), channel_id=1, source_target_pairs={{1,0},{3,2},{5,4},{7,6},{9,8},{11,10},{13,12},{15,14},{17,16},{19,... | collective-permute-start | bytes 2162696 | tf_op jit(solution)/shard_map/ppermute | solution.py:17
  49.3 158.3 %collective-permute-start.2 = (f32[42,1,1,3,128,128]{5,4,0,3,2,1:T(8,128)}, f32[42,1,1,3,128,128]{5,4,0,3,2,1:T(8,128)}, u32[]{:S(2)}, u32[]{:S(2)}) collective-permute-start(f32[42,1,1,3,128,128]{5,4,0,3,2,1:T(8,128)} %fusion.7), channel_id=1, source_target_pairs={{0,8},{8,16},{16,24},{24,0},{1,9},{9,17},{17,25},{25,1},{2,10},{10... | collective-permute-start | bytes 24772616 | tf_op jit(solution)/shard_map/ppermute | solution.py:55
  49.9 46.9 %slice-start.2 = ((s8[20971520]{0:T(1024)(128)(4,1)}), s8[4194304]{0:T(1024)(128)(4,1)S(1)}, s32[]{:S(2)}) async-start(s8[20971520]{0:T(1024)(128)(4,1)} %bitcast.492), calls=%async_computation.3 | async-start | bytes 8388608
  49.9 46.8 %slice-start.3 = ((s8[20971520]{0:T(1024)(128)(4,1)}), s8[4194304]{0:T(1024)(128)(4,1)S(1)}, s32[]{:S(2)}) async-start(s8[20971520]{0:T(1024)(128)(4,1)} %bitcast.492), calls=%async_computation.4 | async-start | bytes 8388608
  49.9 46.8 %slice-start.4 = ((s8[20971520]{0:T(1024)(128)(4,1)}), s8[4194304]{0:T(1024)(128)(4,1)S(1)}, s32[]{:S(2)}) async-start(s8[20971520]{0:T(1024)(128)(4,1)} %bitcast.492), calls=%async_computation.5 | async-start | bytes 8388608
  70.8 33.7 %slice-start.12 = ((s8[7864320]{0:T(1024)(128)(4,1)}), s8[4194304]{0:T(1024)(128)(4,1)S(1)}, s32[]{:S(2)}) async-start(s8[7864320]{0:T(1024)(128)(4,1)} %bitcast.496), calls=%async_computation.13 | async-start | bytes 8388608
  78.7 18.0 %slice-start.5 = ((s8[20971520]{0:T(1024)(128)(4,1)}), s8[4194304]{0:T(1024)(128)(4,1)S(1)}, s32[]{:S(2)}) async-start(s8[20971520]{0:T(1024)(128)(4,1)} %bitcast.492), calls=%async_computation.6 | async-start | bytes 8388608
  78.7 18.0 %slice-start.6 = ((s8[20971520]{0:T(1024)(128)(4,1)}), s8[4194304]{0:T(1024)(128)(4,1)S(1)}, s32[]{:S(2)}) async-start(s8[20971520]{0:T(1024)(128)(4,1)} %bitcast.492), calls=%async_computation.7 | async-start | bytes 8388608
  78.7 25.8 %slice-start.13 = ((s8[7864320]{0:T(1024)(128)(4,1)}), s8[3670016]{0:T(1024)(128)(4,1)S(1)}, s32[]{:S(2)}) async-start(s8[7864320]{0:T(1024)(128)(4,1)} %bitcast.496), calls=%async_computation.14 | async-start | bytes 7340032
  190.1 223.0 %collective-permute-start.3 = (f32[42,1,1,3,128,128]{5,4,0,3,2,1:T(8,128)}, f32[42,1,1,3,128,128]{5,4,0,3,2,1:T(8,128)}, u32[]{:S(2)}, u32[]{:S(2)}) collective-permute-start(f32[42,1,1,3,128,128]{5,4,0,3,2,1:T(8,128)} %fusion.7), channel_id=1, source_target_pairs={{0,24},{8,0},{16,8},{24,16},{1,25},{9,1},{17,9},{25,17},{2,26},{10... | collective-permute-start | bytes 24772616 | tf_op jit(solution)/shard_map/ppermute | solution.py:60
  207.6 226.4 %collective-permute-start.4 = (f32[42,1,1,3,128,128]{5,4,0,3,2,1:T(8,128)}, f32[42,1,1,3,128,128]{5,4,0,3,2,1:T(8,128)}, u32[]{:S(2)}, u32[]{:S(2)}) collective-permute-start(f32[42,1,1,3,128,128]{5,4,0,3,2,1:T(8,128)} %collective-permute-done.2), channel_id=1, source_target_pairs={{0,8},{8,16},{16,24},{24,0},{1,9},{9,17},{17,25},{25,1},{2,10},{10... | collective-permute-start | bytes 24772616 | tf_op jit(solution)/shard_map/ppermute | solution.py:55
  255.5 24.5 %slice-start.7 = ((s8[20971520]{0:T(1024)(128)(4,1)}), s8[4194304]{0:T(1024)(128)(4,1)S(1)}, s32[]{:S(2)}) async-start(s8[20971520]{0:T(1024)(128)(4,1)} %bitcast.494), calls=%async_computation.8 | async-start | bytes 8388608
  255.5 24.5 %slice-start.8 = ((s8[20971520]{0:T(1024)(128)(4,1)}), s8[4194304]{0:T(1024)(128)(4,1)S(1)}, s32[]{:S(2)}) async-start(s8[20971520]{0:T(1024)(128)(4,1)} %bitcast.494), calls=%async_computation.9 | async-start | bytes 8388608
  255.5 24.5 %slice-start.9 = ((s8[20971520]{0:T(1024)(128)(4,1)}), s8[4194304]{0:T(1024)(128)(4,1)S(1)}, s32[]{:S(2)}) async-start(s8[20971520]{0:T(1024)(128)(4,1)} %bitcast.494), calls=%async_computation.10 | async-start | bytes 8388608
  255.5 24.5 %slice-start.10 = ((s8[20971520]{0:T(1024)(128)(4,1)}), s8[4194304]{0:T(1024)(128)(4,1)S(1)}, s32[]{:S(2)}) async-start(s8[20971520]{0:T(1024)(128)(4,1)} %bitcast.494), calls=%async_computation.11 | async-start | bytes 8388608
  280.1 15.5 %slice-start = ((s8[7864320]{0:T(1024)(128)(4,1)}), s8[4194304]{0:T(1024)(128)(4,1)S(1)}, s32[]{:S(2)}) async-start(s8[7864320]{0:T(1024)(128)(4,1)} %bitcast.476), calls=%async_computation.1 | async-start | bytes 8388608
  623.1 34.2 %slice-start.14 = ((s8[10485760]{0:T(1024)(128)(4,1)}), s8[2097152]{0:T(1024)(128)(4,1)S(1)}, s32[]{:S(2)}) async-start(s8[10485760]{0:T(1024)(128)(4,1)} %bitcast.498), calls=%async_computation.15 | async-start | bytes 4194304
  623.1 34.2 %slice-start.15 = ((s8[10485760]{0:T(1024)(128)(4,1)}), s8[4194304]{0:T(1024)(128)(4,1)S(1)}, s32[]{:S(2)}) async-start(s8[10485760]{0:T(1024)(128)(4,1)} %bitcast.498), calls=%async_computation.16 | async-start | bytes 8388608
  637.8 19.4 %slice-start.16 = ((s8[10485760]{0:T(1024)(128)(4,1)}), s8[4194304]{0:T(1024)(128)(4,1)S(1)}, s32[]{:S(2)}) async-start(s8[10485760]{0:T(1024)(128)(4,1)} %bitcast.498), calls=%async_computation.17 | async-start | bytes 8388608
  637.8 19.4 %copy-start.4 = (f32[40,128,128,1]{1,2,3,0:T(8,128)S(1)}, f32[40,128,128,1]{1,2,3,0:T(8,128)}, u32[]{:S(2)}) copy-start(f32[40,128,128,1]{1,2,3,0:T(8,128)} %fusion.4) | copy-start | bytes 7864324
  (6 other events, 57.1 us)
Sparse Core Ops, SparseCore 0:
  15.4 529.8 all-gather.1
